TPU v7x, 32 devices: a whole 2x2x4 slice. The times are simulated.
32 devices in a mesh: grp: 2 (over y), row: 4 (over z), col: 4 (over x, core).
Axes of the slice: x: 2, y: 2, z: 4, core: 2. Of those that a mesh axis runs over, the one named last changes fastest.
Arguments:
- factor: float32 [4, 1024, 1024], P('grp', ('row', 'col')), may hold values from -0.1875 to 0.1875
- pivots: float32 [4, 1024], P('grp', ('row', 'col')), may hold values from 0.5 to 2
- constraints: float32 [4, 1024, 4096], P('grp', None, ('col', 'row')), may hold values from -0.09375 to 0.09375
Outputs:
- q_panels: float32 [4, 1024, 4096], P('row', 'grp', 'col')
All inputs are finite; a program needn't handle non-finite values.
Results may differ from a plain program's by a relative error of at most 0.0011.
Values may be sent and summed in bfloat16 or wider, within the bound.
A program may use at most 64 MiB of HBM per device.

v0:
```python
import jax
import jax.numpy as jnp
from jax import lax
from jax.sharding import PartitionSpec as P

exact_mode = lax.Precision.HIGHEST


def body(factor, pivots, constraints):
    factor_piece = lax.all_gather(factor, ("row", "col"), axis=1, tiled=True)
    pivot_piece = lax.all_gather(pivots, ("row", "col"), axis=1, tiled=True)
    row_ids = lax.broadcasted_iota(jnp.int32, factor_piece.shape, 1)
    col_ids = lax.broadcasted_iota(jnp.int32, factor_piece.shape, 2)
    triangle = jnp.where(col_ids < row_ids, factor_piece, jnp.zeros_like(factor_piece))
    product = jnp.einsum(
        "brm,bms->brs",
        triangle,
        constraints,
        precision=exact_mode,
        preferred_element_type=jnp.float32,
    )
    scaled = pivot_piece[:, :, None] * constraints
    projected_full = product + scaled
    projected = projected_full.astype(jnp.bfloat16)
    column_panel = lax.all_gather(projected, "row", axis=2, tiled=True)
    gram_tile = lax.dot_general(
        lax.all_gather(projected, "col", axis=2, tiled=True),
        column_panel,
        (((0, 1), (0, 1)), ((), ())),
        preferred_element_type=jnp.float32,
    )
    summed = lax.psum_scatter(gram_tile, "grp", scatter_dimension=0, tiled=True)
    return summed[None]


def solution(mesh):
    in_specs = (
        P("grp", ("row", "col"), None),
        P("grp", ("row", "col")),
        P("grp", None, ("col", "row")),
    )
    out_specs = P("row", "grp", "col")
    return jax.shard_map(body, mesh=mesh, in_specs=in_specs, out_specs=out_specs, check_vma=False)
```

profile of v0, /device:TPU:0, one launch (start us, length us, event | category | flops | bytes accessed | tf_op | source)
XLA Modules:
  0.0 284.5 jit_solution(2137502294490413980)
XLA Ops:
  6.5 0.0 all-gather.5.cloned.1.call-start
  6.5 0.7 all-gather.5.cloned.1.call-update
  7.3 0.0 all-gather.7.cloned.1.call-start
  7.3 23.4 %all-gather = f32[16,64,2]{1,2,0:T(2,128)S(1)} all-gather(f32[1,64,2]{1,2,0:T(2,128)} %bitcast.13), channel_id=1, replica_groups=mesh['grp'=2,'row'=4,'col'=4] {'row','col'}, dimensions={0}, use_global_device_ids=true | all-gather | bytes 8704 | tf_op jit(solution)/shard_map/all_gather | solution.py:11
  30.8 0.1 reshape.2
  30.8 56.4 %all-gather.5.cloned.1.call-done = f32[2,1024,1024]{2,1,0:T(8,128)} async-done(((f32[2,64,1024]{2,1,0:T(8,128)}), f32[2,1024,1024]{2,1,0:T(8,128)}) %all-gather.5.cloned.1.call-update) | async-done | bytes 8388624 | tf_op jit(solution)/shard_map/all_gather | solution.py:10
  87.2 12.5 %add_convert_fusion = bf16[2,1024,256]{2,1,0:T(8,128)(2,1)} fusion(f32[2,1024,256]{2,1,0:T(8,128)} %param.5, f32[2,1024,1024]{2,1,0:T(8,128)} %all-gather.5.cloned.1.call-done, f32[2,1024]{1,0:T(2,128)S(1)} %bitcast.12), kind=kOutput, calls=%fused_computation.5 | convolution fusion | flops 6448218112 | bytes 11542528 | tf_op jit(solution)/shard_map/brm,bms->brs/dot_general | solution.py:15
  99.7 0.0 all-gather.7.cloned.1.call-update
  99.7 0.0 all-gather.9.cloned.1.call-start
  99.8 0.7 all-gather.9.cloned.1.call-update
  100.5 0.0 reduce-scatter.2.cloned.1.call-start
  100.5 32.6 %all-gather.7.cloned.1.call-done = bf16[2,1024,1024]{2,1,0:T(8,128)(2,1)} async-done(((bf16[2,1024,256]{2,1,0:T(8,128)(2,1)}), bf16[2,1024,1024]{2,1,0:T(8,128)(2,1)}) %all-gather.7.cloned.1.call-update) | async-done | bytes 4194320 | tf_op jit(solution)/shard_map/all_gather | solution.py:27
  133.1 82.2 %all-gather.9.cloned.1.call-done = bf16[2,1024,1024]{2,1,0:T(8,128)(2,1)} async-done(((bf16[2,1024,256]{2,1,0:T(8,128)(2,1)}), bf16[2,1024,1024]{2,1,0:T(8,128)(2,1)}) %all-gather.9.cloned.1.call-update) | async-done | bytes 4194320 | tf_op jit(solution)/shard_map/all_gather | solution.py:25
  215.3 10.0 %convolution_bitcast_fusion = f32[1024,1024]{1,0:T(8,128)} fusion(bf16[2,1024,1024]{2,1,0:T(8,128)(2,1)} %all-gather.7.cloned.1.call-done, bf16[2,1024,1024]{2,1,0:T(8,128)(2,1)} %all-gather.9.cloned.1.call-done), kind=kOutput, calls=%fused_computation.4 | convolution fusion | flops 4294967296 | bytes 12582912 | tf_op jit(solution)/shard_map/dot_general | solution.py:26
  225.3 0.0 reduce-scatter.2.cloned.1.call-update
  225.3 52.7 %reduce-scatter.2.cloned.1.call-done = f32[512,1024]{1,0:T(8,128)} async-done(((f32[1024,1024]{1,0:T(8,128)}), f32[512,1024]{1,0:T(8,128)}) %reduce-scatter.2.cloned.1.call-update) | async-done | bytes 2097168 | tf_op jit(solution)/shard_map/reduce_scatter | solution.py:32
  (1 shorter events, 0.0 us)
Async XLA Ops:
  6.5 80.7 %all-gather.5.cloned.1.call-start = ((), (), s32[]{:S(2)}) async-start(), calls=%async_computation.1 | async-start | bytes 8912896 | tf_op jit(solution)/shard_map/all_gather | solution.py:10
  7.3 125.9 %all-gather.7.cloned.1.call-start = ((), (), s32[]{:S(2)}) async-start(), calls=%async_computation.2 | async-start | bytes 5242880 | tf_op jit(solution)/shard_map/all_gather | solution.py:27
  99.7 115.6 %all-gather.9.cloned.1.call-start = ((), (), s32[]{:S(2)}) async-start(), calls=%async_computation.3 | async-start | bytes 5242880 | tf_op jit(solution)/shard_map/all_gather | solution.py:25
  100.5 177.5 %reduce-scatter.2.cloned.1.call-start = ((), (), s32[]{:S(2)}) async-start(), calls=%async_computation.4 | async-start | bytes 6291456 | tf_op jit(solution)/shard_map/reduce_scatter | solution.py:32
Sparse Core Ops, SparseCore 0:
  9.5 77.6 all-gather.4
  99.8 33.2 all-gather.6
  134.7 80.5 all-gather.8
  225.5 52.4 reduce-scatter.1
where the time goes:
time: 285 us
  waiting for transfers between devices  225 us (79%)
  blocking collectives  23.4 us (8%)
  matrix products  22.5 us (8%)
  between operations  13.1 us (5%)
    all_gather x1, waiting for transfers between devices, body(): column_panel = lax.all_gather(projected, 'row', axis=2, tiled=True)  82.2 us
    all_gather x1, waiting for transfers between devices, body(): factor_piece = lax.all_gather(factor, ('row', 'col'), axis=1, tiled=True)  56.4 us
    reduce_scatter x1, waiting for transfers between devices, body(): summed = lax.psum_scatter(gram_tile, 'grp', scatter_dimension=0, tiled=True)  52.7 us
    all_gather x1, waiting for transfers between devices, body(): lax.all_gather(projected, 'col', axis=2, tiled=True)  32.6 us
    all_gather x1, blocking collectives, body(): pivot_piece = lax.all_gather(pivots, ('row', 'col'), axis=1, tiled=True)  23.4 us
    dot_general x1, matrix products, body(): jnp.einsum('brm,bms->brs', triangle, constraints, precision=exact_mode, p...  12.5 us
    dot_general x1, matrix products, body(): lax.dot_general(lax.all_gather(projected, 'col', axis=2, tiled=True), col...  10 us
  transfers between devices with their start and end apart: 4, of which 4 were waited for; matrix products, arithmetic and copies ran while one was open for 0% of the time, Pallas kernels for 0%

commit v1 on v0

--- a/solution.py
+++ b/solution.py
@@ -1,9 +1,42 @@
+import functools
 import jax
 import jax.numpy as jnp
 from jax import lax
 from jax.sharding import PartitionSpec as P
 
 exact_mode = lax.Precision.HIGHEST
+
+
+def edit_the_weights(xin, peer_axis, along_dim):
+    even, piece_out, r2 = (
+        lax.axis_size(peer_axis),
+        lax.axis_index(peer_axis),
+        xin.shape[along_dim],
+    )
+    xs_all = list(map(lambda k: (k, (k + 1) % even), range(even)))
+    items = list(map(lambda k: (k, (k - 1) % even), range(even)))
+    field_out = jnp.zeros(
+        (*xin.shape[:along_dim], even * r2, *xin.shape[along_dim + 1 :]), xin.dtype
+    )
+    field_out = lax.dynamic_update_slice_in_dim(field_out, xin, piece_out * r2, axis=along_dim)
+    outer = mid_arr = xin
+    res = even // 2
+    dev = 1
+    while dev < res + 1:
+        outer = lax.ppermute(outer, peer_axis, xs_all)
+        field_out = lax.dynamic_update_slice_in_dim(
+            field_out, outer, (piece_out - dev) % even * r2, axis=along_dim
+        )
+        if dev < even - res:
+            mid_arr = lax.ppermute(mid_arr, peer_axis, items)
+            field_out = lax.dynamic_update_slice_in_dim(
+                field_out, mid_arr, (piece_out + dev) % even * r2, axis=along_dim
+            )
+        dev += 1
+    return field_out
+
+
+_direct_kinds = functools.partial(edit_the_weights, peer_axis="row", along_dim=2)
 
 
 def body(factor, pivots, constraints):
@@ -22,7 +55,7 @@
     scaled = pivot_piece[:, :, None] * constraints
     projected_full = product + scaled
     projected = projected_full.astype(jnp.bfloat16)
-    column_panel = lax.all_gather(projected, "row", axis=2, tiled=True)
+    column_panel = _direct_kinds(projected)
     gram_tile = lax.dot_general(
         lax.all_gather(projected, "col", axis=2, tiled=True),
         column_panel,

time: 285 us -> 242 us (0.85)
  waiting for transfers between devices: 225 us -> 175 us
  local copies, waits for them, and re-layouts: 0.08 us -> 5.93 us
  starting transfers between devices: 0.12 us -> 3.96 us
    all_gather x1 -> x0, waiting for transfers between devices: 82.2 us -> none  [body(): column_panel = lax.all_gather(projected, 'row', axis=2, tiled=True)]
    ppermute x0 -> x3, waiting for transfers between devices: none -> 66.3 us  [the longest x2 46.8 us: edit_the_weights(): outer = lax.ppermute(outer, peer_axis, xs_all)]
    all_gather x1, waiting for transfers between devices: 32.6 us -> 0.01 us  [body(): lax.all_gather(projected, 'col', axis=2, tiled=True)]
    ppermute x0 -> x3, starting transfers between devices: none -> 3.88 us  [the longest x1 2.94 us: edit_the_weights(): mid_arr = lax.ppermute(mid_arr, peer_axis, items)]
    dynamic_update_slice x0 -> x3, local copies, waits for them, and re-layouts: none -> 3.35 us  [the longest x2 2.23 us: edit_the_weights(): lax.dynamic_update_slice_in_dim(field_out, outer, (piece_out - dev) % eve...]
  transfers between devices with their start and end apart: 4 -> 6, of which waited for: 4 -> 5; matrix products, arithmetic and copies ran while one was open for 0% -> 1% of each run, Pallas kernels for 0% -> 0%
where the time goes in v1:
time: 242 us
  waiting for transfers between devices  175 us (72%)
  blocking collectives  23.4 us (10%)
  matrix products  20 us (8%)
  between operations  13.1 us (5%)
  local copies, waits for them, and re-layouts  5.93 us (2%)
  starting transfers between devices  3.96 us (2%)
    all_gather x1, waiting for transfers between devices, body(): factor_piece = lax.all_gather(factor, ('row', 'col'), axis=1, tiled=True)  56.4 us
    reduce_scatter x1, waiting for transfers between devices, body(): summed = lax.psum_scatter(gram_tile, 'grp', scatter_dimension=0, tiled=True)  52 us
    ppermute x2, waiting for transfers between devices, edit_the_weights(): outer = lax.ppermute(outer, peer_axis, xs_all)  46.8 us
    all_gather x1, blocking collectives, body(): pivot_piece = lax.all_gather(pivots, ('row', 'col'), axis=1, tiled=True)  23.4 us
    ppermute x1, waiting for transfers between devices, edit_the_weights(): mid_arr = lax.ppermute(mid_arr, peer_axis, items)  19.5 us
    dot_general x1, matrix products, body(): jnp.einsum('brm,bms->brs', triangle, constraints, precision=exact_mode, p...  10.1 us
    dot_general x1, matrix products, body(): lax.dot_general(lax.all_gather(projected, 'col', axis=2, tiled=True), col...  10 us
  transfers between devices with their start and end apart: 6, of which 5 were waited for; matrix products, arithmetic and copies ran while one was open for 1% of the time, Pallas kernels for 0%

profile of v1, /device:TPU:0, one launch (start us, length us, event | category | flops | bytes accessed | tf_op | source)
XLA Modules:
  0.0 241.9 jit_solution(11542675467153753420)
XLA Ops:
  6.5 0.0 copy-start
  6.5 0.0 all-gather.4.cloned.1.call-start
  6.5 0.7 all-gather.4.cloned.1.call-update
  7.3 0.0 all-gather.6.cloned.1.call-start
  7.3 23.4 %all-gather = f32[16,64,2]{1,2,0:T(2,128)S(1)} all-gather(f32[1,64,2]{1,2,0:T(2,128)} %bitcast.13), channel_id=1, replica_groups=mesh['grp'=2,'row'=4,'col'=4] {'row','col'}, dimensions={0}, use_global_device_ids=true | all-gather | bytes 8704 | tf_op jit(solution)/shard_map/all_gather | solution.py:44
  30.8 0.1 reshape.2
  30.8 56.4 %all-gather.4.cloned.1.call-done = f32[2,1024,1024]{2,1,0:T(8,128)} async-done(((f32[2,64,1024]{2,1,0:T(8,128)}), f32[2,1024,1024]{2,1,0:T(8,128)}) %all-gather.4.cloned.1.call-update) | async-done | bytes 8388624 | tf_op jit(solution)/shard_map/all_gather | solution.py:43
  87.2 2.5 %broadcast_in_dim.11 = bf16[2,1024,1024]{2,1,0:T(8,128)(2,1)} broadcast(bf16[]{:T(256)} %constant.31.clone.1), dimensions={} | broadcast | bytes 4194306 | tf_op jit(solution)/shard_map/broadcast_in_dim | solution.py:18
  89.7 0.0 copy-done
  89.7 10.1 %constant_dynamic-update-slice_fusion.3 = (bf16[2,1024,1024]{2,1,0:T(8,128)(2,1)}, bf16[2,1024,256]{2,1,0:T(8,128)(2,1)}) fusion(bf16[2,1024,1024]{2,1,0:T(8,128)(2,1)} %broadcast_in_dim.11, s32[]{:T(128)S(6)} %select_n.32, f32[2,1024,256]{2,1,0:T(8,128)S(1)} %copy-done, f32[2,1024]{1,0:T(2,128)S(1)} %bitcast.12, ...), kind=kOutput, calls=%fused_computation.9 | convolution fusion | flops 6448218112 | bytes 14688260 | tf_op jit(solution)/shard_map/brm,bms->brs/dot_general | solution.py:48
  99.8 0.0 all-gather.6.cloned.1.call-update
  99.8 0.0 reduce-scatter.2.cloned.1.call-start
  99.8 0.9 collective-permute-start
  100.8 2.9 %collective-permute-start.1 = (bf16[2,1024,256]{2,1,0:T(8,128)(2,1)}, bf16[2,1024,256]{2,1,0:T(8,128)(2,1)S(1)}, u32[]{:S(2)}, u32[]{:S(2)}) collective-permute-start(bf16[2,1024,256]{2,1,0:T(8,128)(2,1)} %get-tuple-element.6), channel_id=1, source_target_pairs={{0,12},{4,0},{8,4},{12,8},{1,13},{5,1},{9,5},{13,9},{2,14},{6,2},{... | collective-permute-start | bytes 3145736 | tf_op jit(solution)/shard_map/ppermute | solution.py:31
  103.7 24.2 %collective-permute-done = bf16[2,1024,256]{2,1,0:T(8,128)(2,1)S(1)} collective-permute-done((bf16[2,1024,256]{2,1,0:T(8,128)(2,1)}, bf16[2,1024,256]{2,1,0:T(8,128)(2,1)S(1)}, u32[]{:S(2)}, u32[]{:S(2)}) %collective-permute-start) | collective-permute-done | bytes 1048608 | tf_op jit(solution)/shard_map/ppermute | solution.py:26
  127.9 0.0 collective-permute-start.2
  127.9 1.1 constant_dynamic-update-slice_fusion.2
  129.0 19.5 %collective-permute-done.1 = bf16[2,1024,256]{2,1,0:T(8,128)(2,1)S(1)} collective-permute-done((bf16[2,1024,256]{2,1,0:T(8,128)(2,1)}, bf16[2,1024,256]{2,1,0:T(8,128)(2,1)S(1)}, u32[]{:S(2)}, u32[]{:S(2)}) %collective-permute-start.1) | collective-permute-done | bytes 1048608 | tf_op jit(solution)/shard_map/ppermute | solution.py:31
  148.5 1.1 constant_dynamic-update-slice_fusion.1
  149.6 22.6 %collective-permute-done.2 = bf16[2,1024,256]{2,1,0:T(8,128)(2,1)S(1)} collective-permute-done((bf16[2,1024,256]{2,1,0:T(8,128)(2,1)S(1)}, bf16[2,1024,256]{2,1,0:T(8,128)(2,1)S(1)}, u32[]{:S(2)}, u32[]{:S(2)}) %collective-permute-start.2) | collective-permute-done | bytes 1048608 | tf_op jit(solution)/shard_map/ppermute | solution.py:26
  172.2 1.1 constant_dynamic-update-slice_fusion
  173.3 0.0 all-gather.6.cloned.1.call-done
  173.3 10.0 %convolution_bitcast_fusion = f32[1024,1024]{1,0:T(8,128)} fusion(bf16[2,1024,1024]{2,1,0:T(8,128)(2,1)} %all-gather.6.cloned.1.call-done, bf16[2,1024,1024]{2,1,0:T(8,128)(2,1)} %constant_dynamic-update-slice_fusion), kind=kOutput, calls=%fused_computation.4 | convolution fusion | flops 4294967296 | bytes 12582912 | tf_op jit(solution)/shard_map/dot_general | solution.py:59
  183.3 0.0 reduce-scatter.2.cloned.1.call-update
  183.3 52.0 %reduce-scatter.2.cloned.1.call-done = f32[512,1024]{1,0:T(8,128)} async-done(((f32[1024,1024]{1,0:T(8,128)}), f32[512,1024]{1,0:T(8,128)}) %reduce-scatter.2.cloned.1.call-update) | async-done | bytes 2097168 | tf_op jit(solution)/shard_map/reduce_scatter | solution.py:65
  (1 shorter events, 0.0 us)
Async XLA Ops:
  6.5 83.2 %copy-start = (f32[2,1024,256]{2,1,0:T(8,128)S(1)}, f32[2,1024,256]{2,1,0:T(8,128)}, u32[]{:S(2)}) copy-start(f32[2,1024,256]{2,1,0:T(8,128)} %param.5) | copy-start | bytes 6291460
  6.5 80.7 %all-gather.4.cloned.1.call-start = ((), (), s32[]{:S(2)}) async-start(), calls=%async_computation.1 | async-start | bytes 8912896 | tf_op jit(solution)/shard_map/all_gather | solution.py:43
  7.3 166.1 %all-gather.6.cloned.1.call-start = ((), (), s32[]{:S(2)}) async-start(), calls=%async_computation.2 | async-start | bytes 5242880 | tf_op jit(solution)/shard_map/all_gather | solution.py:60
  99.8 135.5 %reduce-scatter.2.cloned.1.call-start = ((), (), s32[]{:S(2)}) async-start(), calls=%async_computation.3 | async-start | bytes 6291456 | tf_op jit(solution)/shard_map/reduce_scatter | solution.py:65
  99.8 28.1 %collective-permute-start = (bf16[2,1024,256]{2,1,0:T(8,128)(2,1)}, bf16[2,1024,256]{2,1,0:T(8,128)(2,1)S(1)}, u32[]{:S(2)}, u32[]{:S(2)}) collective-permute-start(bf16[2,1024,256]{2,1,0:T(8,128)(2,1)} %get-tuple-element.6), channel_id=1, source_target_pairs={{0,4},{4,8},{8,12},{12,0},{1,5},{5,9},{9,13},{13,1},{2,6},{6,10},{... | collective-permute-start | bytes 3145736 | tf_op jit(solution)/shard_map/ppermute | solution.py:26
  100.8 47.7 %collective-permute-start.1 = (bf16[2,1024,256]{2,1,0:T(8,128)(2,1)}, bf16[2,1024,256]{2,1,0:T(8,128)(2,1)S(1)}, u32[]{:S(2)}, u32[]{:S(2)}) collective-permute-start(bf16[2,1024,256]{2,1,0:T(8,128)(2,1)} %get-tuple-element.6), channel_id=1, source_target_pairs={{0,12},{4,0},{8,4},{12,8},{1,13},{5,1},{9,5},{13,9},{2,14},{6,2},{... | collective-permute-start | bytes 3145736 | tf_op jit(solution)/shard_map/ppermute | solution.py:31
  127.9 44.3 %collective-permute-start.2 = (bf16[2,1024,256]{2,1,0:T(8,128)(2,1)S(1)}, bf16[2,1024,256]{2,1,0:T(8,128)(2,1)S(1)}, u32[]{:S(2)}, u32[]{:S(2)}) collective-permute-start(bf16[2,1024,256]{2,1,0:T(8,128)(2,1)S(1)} %collective-permute-done), channel_id=1, source_target_pairs={{0,4},{4,8},{8,12},{12,0},{1,5},{5,9},{9,13},{13,1},{2,6},{6,10},{... | collective-permute-start | bytes 3145736 | tf_op jit(solution)/shard_map/ppermute | solution.py:26
Sparse Core Ops, SparseCore 0:
  9.5 77.6 all-gather.3
  99.9 33.2 all-gather.5
  183.5 51.8 reduce-scatter.1
